TPU v7x, 32 devices: a whole 2x2x4 slice. The times are simulated.
32 devices in a mesh: row: 8 (over y, x, core), col: 4 (over z).
Axes of the slice: x: 2, y: 2, z: 4, core: 2. Of those that a mesh axis runs over, the one named last changes fastest.
Arguments:
- pair: bfloat16 [64, 64, 128], P('row', 'col'), may hold values from -6 to 6
- pair_mask: int32 [64, 64], P('row', 'col'), may hold values 0 or 1
- ln_in_gain: float32 [128], replicated, may hold values from 0.1 to 1.9
- ln_in_bias: float32 [128], replicated, may hold values from -3 to 3
- w_proj: bfloat16 [128, 512], replicated, may hold values from -0.5 to 0.5
- b_proj: float32 [512], replicated, may hold values from -3 to 3
- w_gate: bfloat16 [128, 128], replicated, may hold values from -0.5 to 0.5
- b_gate: float32 [128], replicated, may hold values from -3 to 3
- ln_mid_gain: float32 [128], replicated, may hold values from 0.1 to 1.9
- ln_mid_bias: float32 [128], replicated, may hold values from -3 to 3
- w_out: bfloat16 [128, 128], replicated, may hold values from -0.5 to 0.5
- b_out: float32 [128], replicated, may hold values from -3 to 3
- cotangent: bfloat16 [64, 64, 128], P('row', 'col'), may hold values from -6 to 6
Outputs:
- update: bfloat16 [64, 64, 128], P('row', 'col')
- pair_grad: float32 [64, 64, 128], P('row', 'col')
All inputs are finite; a program needn't handle non-finite values. No bound on the sum of `pair_mask` on one device may be relied on, other than what follows from the above.
Results may differ from a plain program's by a relative error of at most 0.019.
Values may be sent and summed in bfloat16 or wider, within the bound.
A program may use at most 64 MiB of HBM per device.

v0:
```python
import jax
import jax.numpy as jnp
from jax import lax
from jax.sharding import PartitionSpec as P


def layer_norm(values, gain_vec, bias_vec):
    average = jnp.mean(values, -1, keepdims=True)
    centred = values - average
    inv_std = lax.rsqrt(jnp.mean(centred * centred, -1, keepdims=True) + 1e-05)
    hat_val = centred * inv_std
    return (hat_val * gain_vec + bias_vec, hat_val, inv_std)


def norm_back(upstream, hat_val, inv_std, gain_vec):
    scaled = upstream * gain_vec
    return inv_std * (
        scaled
        - jnp.mean(scaled, -1, keepdims=True)
        - hat_val * jnp.mean(scaled * hat_val, -1, keepdims=True)
    )


def gate_pair(proj, mask_f):
    hidden = proj.shape[-1] // 4
    sig_a = jax.nn.sigmoid(proj[..., :hidden])
    sig_b = jax.nn.sigmoid(proj[..., 2 * hidden : 3 * hidden])
    a_bf = (mask_f * sig_a * proj[..., hidden : 2 * hidden]).astype(jnp.bfloat16)
    b_bf = (mask_f * sig_b * proj[..., 3 * hidden :]).astype(jnp.bfloat16)
    return (a_bf, b_bf)


def gate_back(grad_a, grad_b, proj, mask_f):
    hidden = proj.shape[-1] // 4
    sig_a = jax.nn.sigmoid(proj[..., :hidden])
    val_a = proj[..., hidden : 2 * hidden]
    sig_b = jax.nn.sigmoid(proj[..., 2 * hidden : 3 * hidden])
    val_b = proj[..., 3 * hidden :]
    masked_a = grad_a * mask_f
    masked_b = grad_b * mask_f
    return jnp.concatenate(
        [
            masked_a * val_a * sig_a * (1.0 - sig_a),
            masked_a * sig_a,
            masked_b * val_b * sig_b * (1.0 - sig_b),
            masked_b * sig_b,
        ],
        -1,
    )


def per_device(
    pair,
    pair_mask,
    ln_in_gain,
    ln_in_bias,
    w_proj,
    b_proj,
    w_gate,
    b_gate,
    ln_mid_gain,
    ln_mid_bias,
    w_out,
    b_out,
    cotangent,
):
    normed, hat_in, rstd_in = layer_norm(pair.astype(jnp.float32), ln_in_gain, ln_in_bias)
    x_bf = normed.astype(jnp.bfloat16)
    proj = jnp.dot(x_bf, w_proj, preferred_element_type=jnp.float32) + b_proj
    mask_f = pair_mask.astype(jnp.float32)[..., None]
    a_bf, b_bf = gate_pair(proj, mask_f)
    b_every = lax.all_gather(b_bf, "row", axis=0, tiled=True)
    owned = lax.psum_scatter(
        jnp.einsum("jkh,ikh->jih", b_every, a_bf, preferred_element_type=jnp.float32).astype(
            jnp.bfloat16
        ),
        "col",
        scatter_dimension=0,
        tiled=True,
    ).astype(jnp.float32)
    triangle = jnp.transpose(owned, (1, 0, 2))
    mid_val, hat_mid, rstd_mid = layer_norm(triangle, ln_mid_gain, ln_mid_bias)
    mid_bf = mid_val.astype(jnp.bfloat16)
    out_lin = jnp.dot(mid_bf, w_out, preferred_element_type=jnp.float32) + b_out
    gate = jax.nn.sigmoid(jnp.dot(x_bf, w_gate, preferred_element_type=jnp.float32) + b_gate)
    update = (gate * out_lin).astype(jnp.bfloat16)
    grad_out = cotangent.astype(jnp.float32)
    d_out = (grad_out * gate).astype(jnp.bfloat16)
    d_gpre = (grad_out * out_lin * gate * (1.0 - gate)).astype(jnp.bfloat16)
    d_mid = jnp.dot(d_out, w_out.T, preferred_element_type=jnp.float32)
    d_tri = norm_back(d_mid, hat_mid, rstd_mid, ln_mid_gain).astype(jnp.bfloat16)
    tri_rows = lax.all_gather(d_tri, "col", axis=1, tiled=True)
    grad_a = jnp.einsum("ijh,jkh->ikh", tri_rows, b_every, preferred_element_type=jnp.float32)
    grad_b = lax.psum_scatter(
        jnp.einsum("ijh,ikh->jkh", tri_rows, a_bf, preferred_element_type=jnp.float32).astype(
            jnp.bfloat16
        ),
        "row",
        scatter_dimension=0,
        tiled=True,
    ).astype(jnp.float32)
    d_proj = gate_back(grad_a, grad_b, proj, mask_f).astype(jnp.bfloat16)
    d_x = jnp.dot(d_proj, w_proj.T, preferred_element_type=jnp.float32) + jnp.dot(
        d_gpre, w_gate.T, preferred_element_type=jnp.float32
    )
    pair_grad = norm_back(d_x, hat_in, rstd_in, ln_in_gain)
    return (update, pair_grad)


def solution(mesh):
    placed = (
        P("row", "col", None),
        P("row", "col"),
        P(),
        P(),
        P(),
        P(),
        P(),
        P(),
        P(),
        P(),
        P(),
        P(),
        P("row", "col", None),
    )
    return jax.shard_map(
        per_device,
        mesh=mesh,
        in_specs=placed,
        out_specs=(P("row", "col", None), P("row", "col", None)),
        check_vma=False,
    )
```

profile of v0, /device:TPU:0, one launch (start us, length us, event | category | flops | bytes accessed | tf_op | source)
XLA Modules:
  0.0 108.7 jit_solution(9767718973377871491)
XLA Ops:
  7.2 0.7 convert_element_type.52
  7.9 0.8 convert_reduce_fusion
  8.8 0.9 fusion.26
  9.8 1.0 convolution_add_fusion
  10.9 10.8 %all_gather.6 = bf16[64,16,128]{2,1,0:T(8,128)(2,1)S(1)} all-gather(bf16[8,16,128]{2,1,0:T(8,128)(2,1)S(1)} %get-tuple-element.12), channel_id=1, replica_groups=mesh['row'=8,'col'=4] {'row'}, dimensions={0}, use_global_device_ids=true | all-gather | bytes 294912 | tf_op jit(solution)/shard_map/all_gather | solution.py:72
  21.8 3.0 %copy.24 = bf16[64,16,128]{1,0,2:T(8,128)(2,1)S(1)} copy(bf16[64,16,128]{2,1,0:T(8,128)(2,1)S(1)} %all_gather.6) | data formatting | bytes 524288 | tf_op jit(solution)/shard_map/all_gather | solution.py:72
  24.9 1.2 %fusion = bf16[64,8,128]{0,1,2:T(8,128)(2,1)S(1)} fusion(bf16[8,16,128]{1,0,2:T(8,128)(2,1)S(1)} %copy.23, bf16[64,16,128]{1,0,2:T(8,128)(2,1)S(1)} %copy.24), kind=kOutput, calls=%fused_computation.1 | convolution fusion | flops 2162688 | bytes 425984 | tf_op jit(solution)/shard_map/jkh,ikh->jih/dot_general | solution.py:74
  26.1 0.9 copy.25
  27.0 19.6 %reduce-scatter.3.cloned.1.call-done = bf16[16,8,128]{2,1,0:T(8,128)(2,1)} async-done(((bf16[64,8,128]{2,1,0:T(8,128)(2,1)}), bf16[16,8,128]{2,1,0:T(8,128)(2,1)}) %reduce-scatter.3.cloned.1.call-update) | async-done | bytes 32784 | tf_op jit(solution)/shard_map/reduce_scatter | solution.py:73
  46.7 0.8 bitcast_reduce_fusion
  47.5 0.9 fusion.48
  48.5 1.0 convolution_add_fusion.2
  49.5 0.9 multiply_convert_fusion.4
  50.4 1.0 fusion.67
  51.4 0.9 fusion.47
  52.4 13.4 %all_gather.7 = bf16[8,64,128]{2,0,1:T(8,128)(2,1)S(1)} all-gather(bf16[8,16,128]{2,0,1:T(8,128)(2,1)S(1)} %copy.27), channel_id=1, replica_groups=mesh['row'=8,'col'=4] {'col'}, dimensions={1}, use_global_device_ids=true | all-gather | bytes 163840 | tf_op jit(solution)/shard_map/all_gather | solution.py:92
  65.8 0.2 copy.29
  66.0 0.4 fusion.69
  66.4 1.3 %copy.33 = bf16[128,16,64]{0,1,2:T(8,128)(2,1)} copy(bf16[128,16,64]{2,1,0:T(8,128)(2,1)S(1)} %fusion.69) | data formatting | bytes 524288 | tf_op jit(solution)/shard_map/ijh,ikh->jkh/dot_general | solution.py:95
  67.7 0.7 fusion.68
  68.6 31.1 %reduce-scatter.5.cloned.1.call-done = bf16[8,16,128]{2,1,0:T(8,128)(2,1)} async-done(((bf16[64,16,128]{2,1,0:T(8,128)(2,1)}), bf16[8,16,128]{2,1,0:T(8,128)(2,1)}) %reduce-scatter.5.cloned.1.call-update) | async-done | bytes 32784 | tf_op jit(solution)/shard_map/reduce_scatter | solution.py:94
  99.7 0.9 multiply_convert_fusion.3
  100.8 0.3 fusion.66
  101.1 0.8 fusion.25
  (52 shorter events, 0.9 us)
Async XLA Ops:
  7.2 2.6 %copy-start = (bf16[128,512]{1,0:T(8,128)(2,1)S(1)}, bf16[128,512]{1,0:T(8,128)(2,1)}, u32[]{:S(2)}) copy-start(bf16[128,512]{1,0:T(8,128)(2,1)} %param.17) | copy-start | bytes 393220
  7.2 39.5 %reduce-scatter.3.cloned.1.call-start = ((), (), s32[]{:S(2)}) async-start(), calls=%async_computation.2 | async-start | bytes 163840 | tf_op jit(solution)/shard_map/reduce_scatter | solution.py:73
  24.8 23.7 %copy-start.9 = (bf16[128,128]{1,0:T(8,128)(2,1)S(1)}, bf16[128,128]{1,0:T(8,128)(2,1)}, u32[]{:S(2)}) copy-start(bf16[128,128]{1,0:T(8,128)(2,1)} %param.23) | copy-start | bytes 98308
  24.8 23.7 %copy-start.14 = (f32[128]{0:T(128)S(1)}, f32[128]{0:T(128)}, u32[]{:S(2)}) copy-start(f32[128]{0:T(128)} %param.21) | copy-start | bytes 1540
  24.8 23.7 %copy-start.15 = (f32[128]{0:T(128)S(1)}, f32[128]{0:T(128)}, u32[]{:S(2)}) copy-start(f32[128]{0:T(128)} %param.24) | copy-start | bytes 1540
  24.8 23.7 %copy-start.16 = (f32[128]{0:T(128)S(1)}, f32[128]{0:T(128)}, u32[]{:S(2)}) copy-start(f32[128]{0:T(128)} %param.22) | copy-start | bytes 1540
  24.8 24.6 %copy-start.1 = (bf16[8,16,128]{2,1,0:T(8,128)(2,1)S(1)}, bf16[8,16,128]{2,1,0:T(8,128)(2,1)}, u32[]{:S(2)}) copy-start(bf16[8,16,128]{2,1,0:T(8,128)(2,1)} %param.13) | copy-start | bytes 98308
  24.9 24.6 %copy-start.10 = (bf16[128,128]{1,0:T(8,128)(2,1)S(1)}, bf16[128,128]{1,0:T(8,128)(2,1)}, u32[]{:S(2)}) copy-start(bf16[128,128]{1,0:T(8,128)(2,1)} %param.19) | copy-start | bytes 98308
  24.9 24.6 %copy-start.12 = (f32[128]{0:T(128)S(1)}, f32[128]{0:T(128)}, u32[]{:S(2)}) copy-start(f32[128]{0:T(128)} %param.15) | copy-start | bytes 1540
  24.9 24.6 %copy-start.13 = (f32[128]{0:T(128)S(1)}, f32[128]{0:T(128)}, u32[]{:S(2)}) copy-start(f32[128]{0:T(128)} %param.16) | copy-start | bytes 1540
  24.9 24.6 %copy-start.17 = (f32[128]{0:T(128)S(1)}, f32[128]{0:T(128)}, u32[]{:S(2)}) copy-start(f32[128]{0:T(128)} %param.20) | copy-start | bytes 1540
  24.9 25.5 %copy-start.5 = (bf16[8,16,128]{2,1,0:T(8,128)(2,1)S(1)}, bf16[8,16,128]{2,1,0:T(8,128)(2,1)}, u32[]{:S(2)}) copy-start(bf16[8,16,128]{2,1,0:T(8,128)(2,1)} %param.25) | copy-start | bytes 98308
  27.0 72.7 %reduce-scatter.5.cloned.1.call-start = ((), (), s32[]{:S(2)}) async-start(), calls=%async_computation.3 | async-start | bytes 294912 | tf_op jit(solution)/shard_map/reduce_scatter | solution.py:94
  49.5 0.9 copy-start.7
  50.4 2.0 %copy-start.3 = (f32[8,16,128]{2,1,0:T(8,128)}, f32[8,16,128]{2,1,0:T(8,128)S(1)}, u32[]{:S(2)}) copy-start(f32[8,16,128]{2,1,0:T(8,128)S(1)} %get-tuple-element.15) | copy-start | bytes 196612
  67.7 33.0 %copy-start.2 = (bf16[8,16,128]{2,1,0:T(8,128)(2,1)S(1)}, bf16[8,16,128]{2,1,0:T(8,128)(2,1)}, u32[]{:S(2)}) copy-start(bf16[8,16,128]{2,1,0:T(8,128)(2,1)} %param.13) | copy-start | bytes 98308
  67.7 33.0 %copy-start.4 = (f32[8,16,128]{2,1,0:T(8,128)S(1)}, f32[8,16,128]{2,1,0:T(8,128)}, u32[]{:S(2)}) copy-start(f32[8,16,128]{2,1,0:T(8,128)} %copy-done.3) | copy-start | bytes 196612
  67.7 33.0 %copy-start.6 = (bf16[8,16,128]{2,1,0:T(8,128)(2,1)S(1)}, bf16[8,16,128]{2,1,0:T(8,128)(2,1)}, u32[]{:S(2)}) copy-start(bf16[8,16,128]{2,1,0:T(8,128)(2,1)} %param.25) | copy-start | bytes 98308
  67.7 33.0 %copy-start.8 = (f32[8,16,128]{2,1,0:T(8,128)S(1)}, f32[8,16,128]{2,1,0:T(8,128)}, u32[]{:S(2)}) copy-start(f32[8,16,128]{2,1,0:T(8,128)} %copy-done.7) | copy-start | bytes 196612
  67.7 33.0 %copy-start.11 = (bf16[128,128]{1,0:T(8,128)(2,1)S(1)}, bf16[128,128]{1,0:T(8,128)(2,1)}, u32[]{:S(2)}) copy-start(bf16[128,128]{1,0:T(8,128)(2,1)} %param.19) | copy-start | bytes 98308
Sparse Core Ops, SparseCore 0:
  27.1 19.4 reduce-scatter.2
  67.8 31.8 reduce-scatter.4
where the time goes:
time: 109 us
  waiting for transfers between devices  50.7 us (47%)
  blocking collectives  24.2 us (22%)
  between operations  14.5 us (13%)
  other arithmetic  6.89 us (6%)
  matrix products  6.53 us (6%)
  local copies, waits for them, and re-layouts  5.81 us (5%)
    reduce_scatter x1, waiting for transfers between devices, per_device(): lax.psum_scatter(jnp.einsum('ijh,ikh->jkh', tri_rows, a_bf, preferred_ele...  31.1 us
    reduce_scatter x1, waiting for transfers between devices, per_device(): lax.psum_scatter(jnp.einsum('jkh,ikh->jih', b_every, a_bf, preferred_elem...  19.6 us
    all_gather x1, blocking collectives, per_device(): tri_rows = lax.all_gather(d_tri, 'col', axis=1, tiled=True)  13.4 us
    all_gather x1, blocking collectives, per_device(): b_every = lax.all_gather(b_bf, 'row', axis=0, tiled=True)  10.8 us
    all_gather x1, local copies, waits for them, and re-layouts, per_device(): b_every = lax.all_gather(b_bf, 'row', axis=0, tiled=True)  2.95 us
  transfers between devices with their start and end apart: 2, of which 2 were waited for; matrix products, arithmetic and copies ran while one was open for 1% of the time, Pallas kernels for 0%

commit v1 on v0

--- a/solution.py
+++ b/solution.py
@@ -1,7 +1,32 @@
+import functools
 import jax
 import jax.numpy as jnp
 from jax import lax
 from jax.sharding import PartitionSpec as P
+
+
+def recast_edges(base_x, axis_tag):
+    x_now = jax.lax.axis_size(axis_tag)
+    v_now = jax.lax.axis_index(axis_tag)
+    known, mixed_arr, newest = (x_now, v_now, base_x.shape[0])
+    arrivals = [(hop_no, (hop_no + 1) % known) for hop_no in range(known)]
+    ledger = [(hop_no, (hop_no - 1) % known) for hop_no in range(known)]
+    ready = jnp.zeros((*base_x.shape[:0], known * newest, *base_x.shape[1:]), base_x.dtype)
+    ready = lax.dynamic_update_slice_in_dim(ready, base_x, mixed_arr * newest, axis=0)
+    z1 = y = base_x
+    arr_now = known // 2
+    for s in range(1, arr_now + 1):
+        z1 = jax.lax.ppermute(z1, axis_tag, arrivals)
+        ready = lax.dynamic_update_slice_in_dim(ready, z1, (mixed_arr - s) % known * newest, axis=0)
+        if s < known - arr_now:
+            y = jax.lax.ppermute(y, axis_tag, ledger)
+            ready = lax.dynamic_update_slice_in_dim(
+                ready, y, (mixed_arr + s) % known * newest, axis=0
+            )
+    return ready
+
+
+wait_pools_up = functools.partial(recast_edges, axis_tag="row")
 
 
 def layer_norm(values, gain_vec, bias_vec):
@@ -69,7 +94,7 @@
     proj = jnp.dot(x_bf, w_proj, preferred_element_type=jnp.float32) + b_proj
     mask_f = pair_mask.astype(jnp.float32)[..., None]
     a_bf, b_bf = gate_pair(proj, mask_f)
-    b_every = lax.all_gather(b_bf, "row", axis=0, tiled=True)
+    b_every = wait_pools_up(b_bf)
     owned = lax.psum_scatter(
         jnp.einsum("jkh,ikh->jih", b_every, a_bf, preferred_element_type=jnp.float32).astype(
             jnp.bfloat16

time: 109 us -> 268 us (2.46)
  local copies, waits for them, and re-layouts: 5.81 us -> 166 us
  blocking collectives: 24.2 us -> 13.4 us
  starting transfers between devices: 0.08 us -> 8.82 us
  waiting for transfers between devices: 50.7 us -> 58.1 us
  matrix products: 6.53 us -> 3.02 us
  other arithmetic: 6.89 us -> 3.99 us
    dynamic_update_slice x0 -> x8, local copies, waits for them, and re-layouts: none -> 157 us  [the longest x4 87.2 us: recast_edges(): lax.dynamic_update_slice_in_dim(ready, z1, (mixed_arr - s) % known * newe...]
    all_gather x1 -> x0, blocking collectives: 10.8 us -> none  [per_device(): b_every = lax.all_gather(b_bf, 'row', axis=0, tiled=True)]
    ppermute x0 -> x7, starting transfers between devices: none -> 8.74 us  [the longest x3 8.23 us: recast_edges(): y = jax.lax.ppermute(y, axis_tag, ledger)]
    ppermute x0 -> x7, waiting for transfers between devices: none -> 4.73 us  [the longest x4 4.6 us: recast_edges(): z1 = jax.lax.ppermute(z1, axis_tag, arrivals)]
    ppermute x0 -> x7, local copies, waits for them, and re-layouts: none -> 3.04 us  [the longest x4 1.74 us: recast_edges(): z1 = jax.lax.ppermute(z1, axis_tag, arrivals)]
    all_gather x1 -> x0, local copies, waits for them, and re-layouts: 2.95 us -> none  [per_device(): b_every = lax.all_gather(b_bf, 'row', axis=0, tiled=True)]
  transfers between devices with their start and end apart: 2 -> 9, of which waited for: 2 -> 7; matrix products, arithmetic and copies ran while one was open for 1% -> 52% of each run, Pallas kernels for 0% -> 0%
where the time goes in v1:
time: 268 us
  local copies, waits for them, and re-layouts  166 us (62%)
  waiting for transfers between devices  58.1 us (22%)
  between operations  14.6 us (5%)
  blocking collectives  13.4 us (5%)
  starting transfers between devices  8.82 us (3%)
  other arithmetic  3.99 us (1%)
  matrix products  3.02 us (1%)
    dynamic_update_slice x4, local copies, waits for them, and re-layouts, recast_edges(): lax.dynamic_update_slice_in_dim(ready, z1, (mixed_arr - s) % known * newe...  87.2 us
    dynamic_update_slice x3, local copies, waits for them, and re-layouts, recast_edges(): lax.dynamic_update_slice_in_dim(ready, y, (mixed_arr + s) % known * newes...  65.4 us
    reduce_scatter x1, waiting for transfers between devices, per_device(): lax.psum_scatter(jnp.einsum('ijh,ikh->jkh', tri_rows, a_bf, preferred_ele...  31.5 us
    reduce_scatter x1, waiting for transfers between devices, per_device(): lax.psum_scatter(jnp.einsum('jkh,ikh->jih', b_every, a_bf, preferred_elem...  21.8 us
    all_gather x1, blocking collectives, per_device(): tri_rows = lax.all_gather(d_tri, 'col', axis=1, tiled=True)  13.4 us
    ppermute x3, starting transfers between devices, recast_edges(): y = jax.lax.ppermute(y, axis_tag, ledger)  8.23 us
  transfers between devices with their start and end apart: 9, of which 7 were waited for; matrix products, arithmetic and copies ran while one was open for 52% of the time, Pallas kernels for 0%

profile of v1, /device:TPU:0, one launch (start us, length us, event | category | flops | bytes accessed | tf_op | source)
XLA Modules:
  0.0 268.0 jit_solution(12103794651261011457)
XLA Ops:
  7.2 0.9 convert_reduce_fusion
  10.5 2.9 %collective-permute-start.1 = (bf16[8,16,128]{2,1,0:T(8,128)(2,1)S(1)}, bf16[8,16,128]{2,1,0:T(8,128)(2,1)S(1)}, u32[]{:S(2)}, u32[]{:S(2)}) collective-permute-start(bf16[8,16,128]{2,1,0:T(8,128)(2,1)S(1)} %get-tuple-element.12), channel_id=1, source_target_pairs={{0,28},{4,0},{8,4},{12,8},{16,12},{20,16},{24,20},{28,24},{1,29},{... | collective-permute-start | bytes 98312 | tf_op jit(solution)/shard_map/ppermute | solution.py:22
  13.5 1.5 collective-permute-done
  15.1 2.6 collective-permute-start.3
  17.7 1.5 collective-permute-done.2
  19.3 2.6 collective-permute-start.5
  21.9 1.5 collective-permute-done.4
  24.3 4.6 %dynamic_update_slice.24 = bf16[64,16,128]{0,1,2:T(8,128)(2,1)S(1)} dynamic-update-slice(bf16[64,16,128]{0,1,2:T(8,128)(2,1)S(1)} %broadcast_in_dim.2, bf16[8,16,128]{0,1,2:T(8,128)(2,1)S(1)} %copy.29, s32[]{:T(128)S(6)} %select_n.55, s32[]{:T(128)} %constant.69.clone.1, s32[]{:T(128)} %constant.69.clone.1) | dynamic-update-slice | bytes 65540 | tf_op jit(solution)/shard_map/dynamic_update_slice | solution.py:15
  29.4 21.8 %dynamic_update_slice.25 = bf16[64,16,128]{0,1,2:T(8,128)(2,1)S(1)} dynamic-update-slice(bf16[64,16,128]{0,1,2:T(8,128)(2,1)S(1)} %dynamic_update_slice.24, bf16[8,16,128]{0,1,2:T(8,128)(2,1)S(1)} %copy.30, s32[]{:T(128)S(6)} %select_n.57, s32[]{:T(128)} %constant.69.clone.1, s32[]{:T(128)} %constant.69.clone.1) | dynamic-update-slice | bytes 65540 | tf_op jit(solution)/shard_map/dynamic_update_slice | solution.py:20
  51.7 21.8 %dynamic_update_slice.26 = bf16[64,16,128]{0,1,2:T(8,128)(2,1)S(1)} dynamic-update-slice(bf16[64,16,128]{0,1,2:T(8,128)(2,1)S(1)} %dynamic_update_slice.25, bf16[8,16,128]{0,1,2:T(8,128)(2,1)S(1)} %copy.31, s32[]{:T(128)S(6)} %select_n.59, s32[]{:T(128)} %constant.69.clone.1, s32[]{:T(128)} %constant.69.clone.1) | dynamic-update-slice | bytes 65540 | tf_op jit(solution)/shard_map/dynamic_update_slice | solution.py:23
  73.9 21.8 %dynamic_update_slice.27 = bf16[64,16,128]{0,1,2:T(8,128)(2,1)S(1)} dynamic-update-slice(bf16[64,16,128]{0,1,2:T(8,128)(2,1)S(1)} %dynamic_update_slice.26, bf16[8,16,128]{0,1,2:T(8,128)(2,1)S(1)} %copy.32, s32[]{:T(128)S(6)} %select_n.61, s32[]{:T(128)} %constant.69.clone.1, s32[]{:T(128)} %constant.69.clone.1) | dynamic-update-slice | bytes 65540 | tf_op jit(solution)/shard_map/dynamic_update_slice | solution.py:20
  96.2 21.8 %dynamic_update_slice.28 = bf16[64,16,128]{0,1,2:T(8,128)(2,1)S(1)} dynamic-update-slice(bf16[64,16,128]{0,1,2:T(8,128)(2,1)S(1)} %dynamic_update_slice.27, bf16[8,16,128]{0,1,2:T(8,128)(2,1)S(1)} %copy.33, s32[]{:T(128)S(6)} %select_n.63, s32[]{:T(128)} %constant.69.clone.1, s32[]{:T(128)} %constant.69.clone.1) | dynamic-update-slice | bytes 65540 | tf_op jit(solution)/shard_map/dynamic_update_slice | solution.py:23
  118.4 21.8 %dynamic_update_slice.29 = bf16[64,16,128]{0,1,2:T(8,128)(2,1)S(1)} dynamic-update-slice(bf16[64,16,128]{0,1,2:T(8,128)(2,1)S(1)} %dynamic_update_slice.28, bf16[8,16,128]{0,1,2:T(8,128)(2,1)S(1)} %copy.34, s32[]{:T(128)S(6)} %select_n.65, s32[]{:T(128)} %constant.69.clone.1, s32[]{:T(128)} %constant.69.clone.1) | dynamic-update-slice | bytes 65540 | tf_op jit(solution)/shard_map/dynamic_update_slice | solution.py:20
  140.7 21.8 %dynamic_update_slice.30 = bf16[64,16,128]{0,1,2:T(8,128)(2,1)S(1)} dynamic-update-slice(bf16[64,16,128]{0,1,2:T(8,128)(2,1)S(1)} %dynamic_update_slice.29, bf16[8,16,128]{0,1,2:T(8,128)(2,1)S(1)} %copy.35, s32[]{:T(128)S(6)} %select_n.67, s32[]{:T(128)} %constant.69.clone.1, s32[]{:T(128)} %constant.69.clone.1) | dynamic-update-slice | bytes 65540 | tf_op jit(solution)/shard_map/dynamic_update_slice | solution.py:23
  163.0 21.8 %dynamic_update_slice.31 = bf16[64,16,128]{0,1,2:T(8,128)(2,1)S(1)} dynamic-update-slice(bf16[64,16,128]{0,1,2:T(8,128)(2,1)S(1)} %dynamic_update_slice.30, bf16[8,16,128]{0,1,2:T(8,128)(2,1)S(1)} %copy.36, s32[]{:T(128)S(6)} %select_n.69, s32[]{:T(128)} %constant.69.clone.1, s32[]{:T(128)} %constant.69.clone.1) | dynamic-update-slice | bytes 65540 | tf_op jit(solution)/shard_map/dynamic_update_slice | solution.py:20
  185.1 0.9 copy.38
  186.0 21.8 %reduce-scatter.3.cloned.1.call-done = bf16[16,8,128]{2,1,0:T(8,128)(2,1)} async-done(((bf16[64,8,128]{2,1,0:T(8,128)(2,1)}), bf16[16,8,128]{2,1,0:T(8,128)(2,1)}) %reduce-scatter.3.cloned.1.call-update) | async-done | bytes 32784 | tf_op jit(solution)/shard_map/reduce_scatter | solution.py:98
  207.9 0.9 bitcast_reduce_fusion
  210.4 0.9 multiply_convert_fusion.4
  211.7 13.4 %all_gather.3 = bf16[8,64,128]{2,0,1:T(8,128)(2,1)S(1)} all-gather(bf16[8,16,128]{2,0,1:T(8,128)(2,1)S(1)} %copy.40), channel_id=1, replica_groups=mesh['row'=8,'col'=4] {'col'}, dimensions={1}, use_global_device_ids=true | all-gather | bytes 163840 | tf_op jit(solution)/shard_map/all_gather | solution.py:117
  225.7 1.3 copy.45
  227.6 31.5 %reduce-scatter.5.cloned.1.call-done = bf16[8,16,128]{2,1,0:T(8,128)(2,1)} async-done(((bf16[64,16,128]{2,1,0:T(8,128)(2,1)}), bf16[8,16,128]{2,1,0:T(8,128)(2,1)}) %reduce-scatter.5.cloned.1.call-update) | async-done | bytes 32784 | tf_op jit(solution)/shard_map/reduce_scatter | solution.py:119
  259.0 0.9 multiply_convert_fusion.3
  260.4 0.8 fusion.25
  (73 shorter events, 10.2 us)
Async XLA Ops:
  7.2 1.8 copy-start
  7.2 0.9 copy-start.1
  7.2 200.7 %reduce-scatter.3.cloned.1.call-start = ((), (), s32[]{:S(2)}) async-start(), calls=%async_computation.2 | async-start | bytes 163840 | tf_op jit(solution)/shard_map/reduce_scatter | solution.py:98
  8.3 0.7 copy-start.6
  9.0 0.7 copy-start.7
  9.0 0.7 copy-start.8
  9.0 0.7 copy-start.9
  10.0 5.0 %collective-permute-start = (bf16[8,16,128]{2,1,0:T(8,128)(2,1)S(1)}, bf16[8,16,128]{2,1,0:T(8,128)(2,1)S(1)}, u32[]{:S(2)}, u32[]{:S(2)}) collective-permute-start(bf16[8,16,128]{2,1,0:T(8,128)(2,1)S(1)} %get-tuple-element.12), channel_id=1, source_target_pairs={{0,4},{4,8},{8,12},{12,16},{16,20},{20,24},{24,28},{28,0},{1,5},{5... | collective-permute-start | bytes 98312 | tf_op jit(solution)/shard_map/ppermute | solution.py:19
  10.5 4.5 %collective-permute-start.1 = (bf16[8,16,128]{2,1,0:T(8,128)(2,1)S(1)}, bf16[8,16,128]{2,1,0:T(8,128)(2,1)S(1)}, u32[]{:S(2)}, u32[]{:S(2)}) collective-permute-start(bf16[8,16,128]{2,1,0:T(8,128)(2,1)S(1)} %get-tuple-element.12), channel_id=1, source_target_pairs={{0,28},{4,0},{8,4},{12,8},{16,12},{20,16},{24,20},{28,24},{1,29},{... | collective-permute-start | bytes 98312 | tf_op jit(solution)/shard_map/ppermute | solution.py:22
  15.0 4.2 %collective-permute-start.2 = (bf16[8,16,128]{2,1,0:T(8,128)(2,1)S(1)}, bf16[8,16,128]{2,1,0:T(8,128)(2,1)S(1)}, u32[]{:S(2)}, u32[]{:S(2)}) collective-permute-start(bf16[8,16,128]{2,1,0:T(8,128)(2,1)S(1)} %collective-permute-done), channel_id=1, source_target_pairs={{0,4},{4,8},{8,12},{12,16},{16,20},{20,24},{24,28},{28,0},{1,5},{5... | collective-permute-start | bytes 98312 | tf_op jit(solution)/shard_map/ppermute | solution.py:19
  15.1 4.2 %collective-permute-start.3 = (bf16[8,16,128]{2,1,0:T(8,128)(2,1)S(1)}, bf16[8,16,128]{2,1,0:T(8,128)(2,1)S(1)}, u32[]{:S(2)}, u32[]{:S(2)}) collective-permute-start(bf16[8,16,128]{2,1,0:T(8,128)(2,1)S(1)} %collective-permute-done.1), channel_id=1, source_target_pairs={{0,28},{4,0},{8,4},{12,8},{16,12},{20,16},{24,20},{28,24},{1,29},{... | collective-permute-start | bytes 98312 | tf_op jit(solution)/shard_map/ppermute | solution.py:22
  19.2 4.2 %collective-permute-start.4 = (bf16[8,16,128]{2,1,0:T(8,128)(2,1)S(1)}, bf16[8,16,128]{2,1,0:T(8,128)(2,1)S(1)}, u32[]{:S(2)}, u32[]{:S(2)}) collective-permute-start(bf16[8,16,128]{2,1,0:T(8,128)(2,1)S(1)} %collective-permute-done.2), channel_id=1, source_target_pairs={{0,4},{4,8},{8,12},{12,16},{16,20},{20,24},{24,28},{28,0},{1,5},{5... | collective-permute-start | bytes 98312 | tf_op jit(solution)/shard_map/ppermute | solution.py:19
  19.3 121.0 %collective-permute-start.5 = (bf16[8,16,128]{2,1,0:T(8,128)(2,1)S(1)}, bf16[8,16,128]{2,1,0:T(8,128)(2,1)S(1)}, u32[]{:S(2)}, u32[]{:S(2)}) collective-permute-start(bf16[8,16,128]{2,1,0:T(8,128)(2,1)S(1)} %collective-permute-done.3), channel_id=1, source_target_pairs={{0,28},{4,0},{8,4},{12,8},{16,12},{20,16},{24,20},{28,24},{1,29},{... | collective-permute-start | bytes 98312 | tf_op jit(solution)/shard_map/ppermute | solution.py:22
  23.5 139.1 %collective-permute-start.6 = (bf16[8,16,128]{2,1,0:T(8,128)(2,1)S(1)}, bf16[8,16,128]{2,1,0:T(8,128)(2,1)S(1)}, u32[]{:S(2)}, u32[]{:S(2)}) collective-permute-start(bf16[8,16,128]{2,1,0:T(8,128)(2,1)S(1)} %collective-permute-done.4), channel_id=1, source_target_pairs={{0,4},{4,8},{8,12},{12,16},{16,20},{20,24},{24,28},{28,0},{1,5},{5... | collective-permute-start | bytes 98312 | tf_op jit(solution)/shard_map/ppermute | solution.py:19
  186.0 73.1 %reduce-scatter.5.cloned.1.call-start = ((), (), s32[]{:S(2)}) async-start(), calls=%async_computation.3 | async-start | bytes 294912 | tf_op jit(solution)/shard_map/reduce_scatter | solution.py:119
  207.9 0.9 copy-start.2
  208.8 0.8 copy-start.4
  209.0 0.7 copy-start.10
  209.0 0.7 copy-start.11
  209.0 0.7 copy-start.12
  209.7 0.8 copy-start.5
  209.7 0.8 copy-start.13
  210.4 0.9 copy-start.3
Sparse Core Ops, SparseCore 0:
  186.1 21.7 reduce-scatter.2
  227.1 31.8 reduce-scatter.4
